TPU v7x, 256 devices: a whole 4x4x8 slice. The times are simulated.
256 devices in a mesh: pipe: 8 (over x, core), expert: 32 (over y, z).
Axes of the slice: x: 4, y: 4, z: 8, core: 2. Of those that a mesh axis runs over, the one named last changes fastest.
Arguments:
- acts: bfloat16 [8, 2, 2048, 2048], P('pipe', None, 'expert'), may hold values from -6 to 6
- out_grad: bfloat16 [2, 2048, 2048], P(None, 'expert'), may hold values from -6 to 6
- w_gate: bfloat16 [8, 32, 2048, 768], P('pipe', 'expert'), may hold values from -0.125 to 0.125
- w_up: bfloat16 [8, 32, 2048, 768], P('pipe', 'expert'), may hold values from -0.125 to 0.125
- w_down: bfloat16 [8, 32, 768, 2048], P('pipe', 'expert'), may hold values from -0.21875 to 0.21875
- routes: int32 [8, 2, 2048, 8], P('pipe', None, 'expert'), may hold values from 0 to 127, all different within a row
- gates: float32 [8, 2, 2048, 8], P('pipe', None, 'expert'), may hold values from 0.2 to 0.6
Outputs:
- in_grad: bfloat16 [8, 2, 2048, 2048], P('pipe', None, 'expert')
Inputs may be any that keep to these rules, and one draw needn't show every extreme that they name: `routes`: each token's 8 choices name different experts, and every expert is chosen somewhere.
All inputs are finite; a program needn't handle non-finite values.
Results may differ from a plain program's by a relative error of at most 0.02.
Values may be sent and summed in bfloat16 or wider, within the bound.
A program may use at most 64 MiB of HBM per device.

v0:
```python
from functools import partial

import jax
import jax.numpy as jnp
from jax import lax
from jax.sharding import PartitionSpec as P

EXPERTS = 128
TOP = 8
CAP = 6


def from_behind(shard, axis, by):
    length = lax.axis_size(axis)
    pairs = [(i, i + by) for i in range(length) if 0 <= i + by < length]
    return lax.ppermute(shard, axis, pairs)


def slot_tables(choose, weigh, live_count):
    choice_list = choose.reshape(-1)
    one_hot = (choice_list[:, None] == jnp.arange(EXPERTS, dtype=jnp.int32)[None, :]).astype(
        jnp.int32
    )
    before = jnp.cumsum(one_hot, axis=0) - one_hot
    slot_index = jnp.sum(before * one_hot, axis=1)
    kept_mask = (choice_list < live_count) & (slot_index < CAP)
    dump_slot = live_count * CAP
    slot_place = jnp.where(kept_mask, choice_list * CAP + slot_index, dump_slot)
    token_index = jnp.arange(choice_list.shape[0], dtype=jnp.int32) // TOP
    holder = jnp.full((dump_slot + 1,), choose.shape[0], jnp.int32).at[slot_place].set(token_index)
    kept_weight = jnp.where(
        kept_mask, weigh.reshape(-1), jnp.zeros_like(weigh.reshape(-1))
    ).reshape(choose.shape)
    return (holder[:dump_slot], slot_place.reshape(choose.shape), kept_weight)


def dispatch_rows(token_block, slot_owner):
    padded = jnp.concatenate(
        [token_block, jnp.zeros((1, token_block.shape[1]), token_block.dtype)], axis=0
    )
    return padded[slot_owner]


def combine_rows(returned, slot_place, kept_weight, incoming):
    padded = jnp.concatenate([returned, jnp.zeros((1, returned.shape[1]), returned.dtype)], axis=0)
    picked = padded[slot_place].astype(jnp.float32)
    summed = incoming.astype(jnp.float32) + jnp.einsum("tkd,tk->td", picked, kept_weight)
    return summed.astype(jnp.bfloat16)


def shards(acts, out_grad, w_gate, w_up, w_down, routes, gates):
    section_count = lax.axis_size("pipe")
    section_index = lax.axis_index("pipe")
    live_count = lax.axis_size("expert")
    last_section = section_count - 1
    section_acts = acts[0]
    gate_matrix = w_gate[0, 0]
    up_matrix = w_up[0, 0]
    down_matrix = w_down[0, 0]
    slot_owner, slot_place, kept_weight = jax.vmap(partial(slot_tables, live_count=live_count))(
        routes[0], gates[0]
    )
    micro_count = section_acts.shape[0]
    group_size = 1
    group_count = micro_count // group_size
    dispatch_all = jax.vmap(dispatch_rows)

    def shaped(slot_rows):
        return slot_rows.reshape(slot_rows.shape[0], live_count, -1, slot_rows.shape[-1])

    def take_group(group_table, group_index):
        return lax.dynamic_slice_in_dim(group_table, group_index * group_size, group_size, 0)

    def backward_rows(gate_pre, up_pre, grad_rows):
        hidden_grad = jnp.einsum(
            "gecd,hd->gech", grad_rows, down_matrix, preferred_element_type=jnp.float32
        )
        sigmoid_gate = jax.nn.sigmoid(gate_pre)
        gate_grad = (
            hidden_grad * up_pre * sigmoid_gate * (1.0 + gate_pre * (1.0 - sigmoid_gate))
        ).astype(jnp.bfloat16)
        up_grad = (hidden_grad * gate_pre * sigmoid_gate).astype(jnp.bfloat16)
        summed = jnp.einsum(
            "gech,dh->gecd", gate_grad, gate_matrix, preferred_element_type=jnp.float32
        )
        summed = summed + jnp.einsum(
            "gech,dh->gecd", up_grad, up_matrix, preferred_element_type=jnp.float32
        )
        return summed.astype(jnp.bfloat16)

    early_acts = shaped(dispatch_all(section_acts, slot_owner))
    slot_rows = lax.all_to_all(early_acts, "expert", split_axis=1, concat_axis=1, tiled=True)
    gate_pre = jnp.einsum(
        "gecd,dh->gech", slot_rows, gate_matrix, preferred_element_type=jnp.float32
    )
    up_pre = jnp.einsum("gecd,dh->gech", slot_rows, up_matrix, preferred_element_type=jnp.float32)
    ahead_gate = gate_pre
    ahead_up = up_pre

    def run_group(group_index, incoming, active):
        owners = take_group(slot_owner, group_index)
        grad_rows = shaped(dispatch_all(incoming, owners))
        arrived_rows = lax.all_to_all(grad_rows, "expert", split_axis=1, concat_axis=1, tiled=True)
        gate_part = take_group(ahead_gate, group_index)
        up_part = take_group(ahead_up, group_index)

        def compute_late(operands):
            return backward_rows(operands[0], operands[1], operands[2])

        def empty_late(operands):
            return jnp.zeros(operands[2].shape, jnp.bfloat16)

        local_rows = lax.cond(active, compute_late, empty_late, (gate_part, up_part, arrived_rows))
        returned = lax.all_to_all(local_rows, "expert", split_axis=1, concat_axis=1, tiled=True)
        flat_back = returned.reshape(group_size, -1, returned.shape[-1])
        combined = jax.vmap(combine_rows)(
            flat_back,
            take_group(slot_place, group_index),
            take_group(kept_weight, group_index),
            incoming,
        )
        return jnp.where(active, combined, jnp.zeros_like(combined))

    def tick_step(tick_index, loop_state):
        arrived, result = loop_state
        group_index = tick_index - (last_section - section_index)
        active = (group_index >= 0) & (group_index < group_count)
        safe_index = jnp.clip(group_index, 0, group_count - 1)
        top_grad = take_group(out_grad, safe_index)
        incoming = jnp.where(section_index == last_section, top_grad, arrived)
        input_grad = run_group(safe_index, incoming, active)
        updated = lax.dynamic_update_slice_in_dim(result, input_grad, safe_index * group_size, 0)
        result = jnp.where(active, updated, result)
        arrived = from_behind(input_grad, "pipe", -1)
        return (arrived, result)

    start_state = (
        jnp.zeros((group_size,) + section_acts.shape[1:], jnp.bfloat16),
        jnp.zeros_like(section_acts),
    )
    final_state = lax.fori_loop(0, section_count + group_count - 1, tick_step, start_state)
    return final_state[1][None]


def solution(mesh):
    return jax.shard_map(
        shards,
        mesh=mesh,
        in_specs=(
            P("pipe", None, "expert", None),
            P(None, "expert", None),
            P("pipe", "expert", None, None),
            P("pipe", "expert", None, None),
            P("pipe", "expert", None, None),
            P("pipe", None, "expert", None),
            P("pipe", None, "expert", None),
        ),
        out_specs=P("pipe", None, "expert", None),
        check_vma=False,
    )
```

profile of v0, /device:TPU:3, one launch (start us, length us, event | category | flops | bytes accessed | tf_op | source)
XLA Modules:
  0.0 900.5 jit_solution(13005467388739339111)
XLA Ops:
  8.4 7.3 gather_fusion.2
  21.0 11.4 %all-to-all-start.2 = ((bf16[2,32,6,2048]{3,0,2,1:T(2,128)(2,1)}), bf16[2,32,6,2048]{3,0,2,1:T(2,128)(2,1)S(1)}, u32[]{:S(2)}, u32[]{:S(2)}) async-start(bf16[2,32,6,2048]{3,0,2,1:T(2,128)(2,1)} %copy.48), calls=%async_computation.2 | async-start | bytes 3145728 | tf_op jit(solution)/shard_map/all_to_all | solution.py:92
  32.5 36.5 %all-to-all-done.2 = bf16[2,32,6,2048]{3,0,2,1:T(2,128)(2,1)S(1)} async-done(((bf16[2,32,6,2048]{3,0,2,1:T(2,128)(2,1)}), bf16[2,32,6,2048]{3,0,2,1:T(2,128)(2,1)S(1)}, u32[]{:S(2)}, u32[]{:S(2)}) %all-to-all-start.2) | async-done | bytes 1572896 | tf_op jit(solution)/shard_map/all_to_all | solution.py:92
  69.0 5.8 fusion.38
  79.4 821.1 %while.17 = (s32[]{:T(128)}, bf16[1,64,2048]{2,1,0:T(8,128)(2,1)S(1)}, bf16[2,64,2048]{2,1,0:T(8,128)(2,1)}, s32[]{:T(128)}, pred[]{:T(512)}, /*index=5*/bf16[2,...) while((s32[]{:T(128)}, ...), condition=%wide.region_7.8_spmd, body=%wide.region_4.7_spmd.sunk | while | flops 1817974272 | bytes 71481360 | solution.py:141
  85.8 7.6 all-to-all-start
  93.5 24.8 %all-to-all-done = bf16[1,32,6,2048]{3,2,0,1:T(8,128)(2,1)S(1)} async-done(((bf16[1,32,6,2048]{3,2,0,1:T(8,128)(2,1)}), bf16[1,32,6,2048]{3,2,0,1:T(8,128)(2,1)S(1)}, u32[]{:S(2)}, u32[]{:S(2)}) %all-to-all-start) | async-done | bytes 786464 | tf_op jit(solution)/shard_map/while/body/eval_jaxpr/all_to_all | solution.py:103
  119.8 8.4 all-to-all-start.1
  128.5 24.5 %all-to-all-done.1 = bf16[1,32,6,2048]{3,2,0,1:T(8,128)(2,1)S(1)} async-done(((bf16[1,32,6,2048]{3,2,0,1:T(8,128)(2,1)}), bf16[1,32,6,2048]{3,2,0,1:T(8,128)(2,1)S(1)}, u32[]{:S(2)}, u32[]{:S(2)}) %all-to-all-start.1) | async-done | bytes 786464 | tf_op jit(solution)/shard_map/while/body/eval_jaxpr/all_to_all | solution.py:114
  153.3 7.8 gather_fusion.1
  162.5 6.9 collective-permute-start
  169.4 5.1 collective-permute-done
  180.9 4.6 all-to-all-start
  185.6 28.1 %all-to-all-done = bf16[1,32,6,2048]{3,2,0,1:T(8,128)(2,1)S(1)} async-done(((bf16[1,32,6,2048]{3,2,0,1:T(8,128)(2,1)}), bf16[1,32,6,2048]{3,2,0,1:T(8,128)(2,1)S(1)}, u32[]{:S(2)}, u32[]{:S(2)}) %all-to-all-start) | async-done | bytes 786464 | tf_op jit(solution)/shard_map/while/body/eval_jaxpr/all_to_all | solution.py:103
  215.2 5.2 all-to-all-start.1
  220.6 24.9 %all-to-all-done.1 = bf16[1,32,6,2048]{3,2,0,1:T(8,128)(2,1)S(1)} async-done(((bf16[1,32,6,2048]{3,2,0,1:T(8,128)(2,1)}), bf16[1,32,6,2048]{3,2,0,1:T(8,128)(2,1)S(1)}, u32[]{:S(2)}, u32[]{:S(2)}) %all-to-all-start.1) | async-done | bytes 786464 | tf_op jit(solution)/shard_map/while/body/eval_jaxpr/all_to_all | solution.py:114
  245.9 7.8 gather_fusion.1
  255.1 6.3 collective-permute-start
  261.4 5.4 collective-permute-done
  273.1 4.8 all-to-all-start
  278.0 28.0 %all-to-all-done = bf16[1,32,6,2048]{3,2,0,1:T(8,128)(2,1)S(1)} async-done(((bf16[1,32,6,2048]{3,2,0,1:T(8,128)(2,1)}), bf16[1,32,6,2048]{3,2,0,1:T(8,128)(2,1)S(1)}, u32[]{:S(2)}, u32[]{:S(2)}) %all-to-all-start) | async-done | bytes 786464 | tf_op jit(solution)/shard_map/while/body/eval_jaxpr/all_to_all | solution.py:103
  307.5 4.9 all-to-all-start.1
  312.7 24.9 %all-to-all-done.1 = bf16[1,32,6,2048]{3,2,0,1:T(8,128)(2,1)S(1)} async-done(((bf16[1,32,6,2048]{3,2,0,1:T(8,128)(2,1)}), bf16[1,32,6,2048]{3,2,0,1:T(8,128)(2,1)S(1)}, u32[]{:S(2)}, u32[]{:S(2)}) %all-to-all-start.1) | async-done | bytes 786464 | tf_op jit(solution)/shard_map/while/body/eval_jaxpr/all_to_all | solution.py:114
  337.9 7.8 gather_fusion.1
  347.1 6.3 collective-permute-start
  361.2 8.1 all-to-all-start
  369.2 27.9 %all-to-all-done = bf16[1,32,6,2048]{3,2,0,1:T(8,128)(2,1)S(1)} async-done(((bf16[1,32,6,2048]{3,2,0,1:T(8,128)(2,1)}), bf16[1,32,6,2048]{3,2,0,1:T(8,128)(2,1)S(1)}, u32[]{:S(2)}, u32[]{:S(2)}) %all-to-all-start) | async-done | bytes 786464 | tf_op jit(solution)/shard_map/while/body/eval_jaxpr/all_to_all | solution.py:103
  398.7 6.1 all-to-all-start.1
  405.1 24.9 %all-to-all-done.1 = bf16[1,32,6,2048]{3,2,0,1:T(8,128)(2,1)S(1)} async-done(((bf16[1,32,6,2048]{3,2,0,1:T(8,128)(2,1)}), bf16[1,32,6,2048]{3,2,0,1:T(8,128)(2,1)S(1)}, u32[]{:S(2)}, u32[]{:S(2)}) %all-to-all-start.1) | async-done | bytes 786464 | tf_op jit(solution)/shard_map/while/body/eval_jaxpr/all_to_all | solution.py:114
  430.4 7.8 gather_fusion.1
  439.6 6.2 collective-permute-start
  445.8 12.9 %collective-permute-done = bf16[1,64,2048]{2,1,0:T(8,128)(2,1)S(1)} collective-permute-done((bf16[1,64,2048]{2,1,0:T(8,128)(2,1)S(1)}, bf16[1,64,2048]{2,1,0:T(8,128)(2,1)S(1)}, u32[]{:S(2)}, u32[]{:S(2)}) %collective-permute-start) | collective-permute-done | bytes 262176 | tf_op jit(solution)/shard_map/while/body/eval_jaxpr/ppermute | solution.py:16
  465.1 4.8 all-to-all-start
  470.0 20.2 %all-to-all-done = bf16[1,32,6,2048]{3,2,0,1:T(8,128)(2,1)S(1)} async-done(((bf16[1,32,6,2048]{3,2,0,1:T(8,128)(2,1)}), bf16[1,32,6,2048]{3,2,0,1:T(8,128)(2,1)S(1)}, u32[]{:S(2)}, u32[]{:S(2)}) %all-to-all-start) | async-done | bytes 786464 | tf_op jit(solution)/shard_map/while/body/eval_jaxpr/all_to_all | solution.py:103
  490.2 8.5 conditional.2
  500.2 5.1 all-to-all-start.1
  505.6 16.7 %all-to-all-done.1 = bf16[1,32,6,2048]{3,2,0,1:T(8,128)(2,1)S(1)} async-done(((bf16[1,32,6,2048]{3,2,0,1:T(8,128)(2,1)}), bf16[1,32,6,2048]{3,2,0,1:T(8,128)(2,1)S(1)}, u32[]{:S(2)}, u32[]{:S(2)}) %all-to-all-start.1) | async-done | bytes 786464 | tf_op jit(solution)/shard_map/while/body/eval_jaxpr/all_to_all | solution.py:114
  522.6 7.8 gather_fusion.1
  533.7 17.4 %collective-permute-done = bf16[1,64,2048]{2,1,0:T(8,128)(2,1)S(1)} collective-permute-done((bf16[1,64,2048]{2,1,0:T(8,128)(2,1)S(1)}, bf16[1,64,2048]{2,1,0:T(8,128)(2,1)S(1)}, u32[]{:S(2)}, u32[]{:S(2)}) %collective-permute-start) | collective-permute-done | bytes 262176 | tf_op jit(solution)/shard_map/while/body/eval_jaxpr/ppermute | solution.py:16
  557.5 5.1 all-to-all-start
  562.7 17.0 %all-to-all-done = bf16[1,32,6,2048]{3,2,0,1:T(8,128)(2,1)S(1)} async-done(((bf16[1,32,6,2048]{3,2,0,1:T(8,128)(2,1)}), bf16[1,32,6,2048]{3,2,0,1:T(8,128)(2,1)S(1)}, u32[]{:S(2)}, u32[]{:S(2)}) %all-to-all-start) | async-done | bytes 786464 | tf_op jit(solution)/shard_map/while/body/eval_jaxpr/all_to_all | solution.py:103
  579.6 8.5 conditional.2
  589.6 5.5 all-to-all-start.1
  595.4 16.0 %all-to-all-done.1 = bf16[1,32,6,2048]{3,2,0,1:T(8,128)(2,1)S(1)} async-done(((bf16[1,32,6,2048]{3,2,0,1:T(8,128)(2,1)}), bf16[1,32,6,2048]{3,2,0,1:T(8,128)(2,1)S(1)}, u32[]{:S(2)}, u32[]{:S(2)}) %all-to-all-start.1) | async-done | bytes 786464 | tf_op jit(solution)/shard_map/while/body/eval_jaxpr/all_to_all | solution.py:114
  611.8 7.8 gather_fusion.1
  622.9 14.0 %collective-permute-done = bf16[1,64,2048]{2,1,0:T(8,128)(2,1)S(1)} collective-permute-done((bf16[1,64,2048]{2,1,0:T(8,128)(2,1)S(1)}, bf16[1,64,2048]{2,1,0:T(8,128)(2,1)S(1)}, u32[]{:S(2)}, u32[]{:S(2)}) %collective-permute-start) | collective-permute-done | bytes 262176 | tf_op jit(solution)/shard_map/while/body/eval_jaxpr/ppermute | solution.py:16
  643.3 4.8 all-to-all-start
  648.1 19.3 %all-to-all-done = bf16[1,32,6,2048]{3,2,0,1:T(8,128)(2,1)S(1)} async-done(((bf16[1,32,6,2048]{3,2,0,1:T(8,128)(2,1)}), bf16[1,32,6,2048]{3,2,0,1:T(8,128)(2,1)S(1)}, u32[]{:S(2)}, u32[]{:S(2)}) %all-to-all-start) | async-done | bytes 786464 | tf_op jit(solution)/shard_map/while/body/eval_jaxpr/all_to_all | solution.py:103
  673.1 25.5 %all-to-all-done.1 = bf16[1,32,6,2048]{3,2,0,1:T(8,128)(2,1)S(1)} async-done(((bf16[1,32,6,2048]{3,2,0,1:T(8,128)(2,1)}), bf16[1,32,6,2048]{3,2,0,1:T(8,128)(2,1)S(1)}, u32[]{:S(2)}, u32[]{:S(2)}) %all-to-all-start.1) | async-done | bytes 786464 | tf_op jit(solution)/shard_map/while/body/eval_jaxpr/all_to_all | solution.py:114
  699.0 7.8 gather_fusion.1
  708.2 5.7 collective-permute-start
  713.8 9.6 %collective-permute-done = bf16[1,64,2048]{2,1,0:T(8,128)(2,1)S(1)} collective-permute-done((bf16[1,64,2048]{2,1,0:T(8,128)(2,1)S(1)}, bf16[1,64,2048]{2,1,0:T(8,128)(2,1)S(1)}, u32[]{:S(2)}, u32[]{:S(2)}) %collective-permute-start) | collective-permute-done | bytes 262176 | tf_op jit(solution)/shard_map/while/body/eval_jaxpr/ppermute | solution.py:16
  729.8 4.8 all-to-all-start
  734.6 24.0 %all-to-all-done = bf16[1,32,6,2048]{3,2,0,1:T(8,128)(2,1)S(1)} async-done(((bf16[1,32,6,2048]{3,2,0,1:T(8,128)(2,1)}), bf16[1,32,6,2048]{3,2,0,1:T(8,128)(2,1)S(1)}, u32[]{:S(2)}, u32[]{:S(2)}) %all-to-all-start) | async-done | bytes 786464 | tf_op jit(solution)/shard_map/while/body/eval_jaxpr/all_to_all | solution.py:103
  760.1 4.8 all-to-all-start.1
  765.2 25.6 %all-to-all-done.1 = bf16[1,32,6,2048]{3,2,0,1:T(8,128)(2,1)S(1)} async-done(((bf16[1,32,6,2048]{3,2,0,1:T(8,128)(2,1)}), bf16[1,32,6,2048]{3,2,0,1:T(8,128)(2,1)S(1)}, u32[]{:S(2)}, u32[]{:S(2)}) %all-to-all-start.1) | async-done | bytes 786464 | tf_op jit(solution)/shard_map/while/body/eval_jaxpr/all_to_all | solution.py:114
  791.1 7.8 gather_fusion.1
  802.2 8.7 collective-permute-done
  817.3 4.8 all-to-all-start
  822.1 22.5 %all-to-all-done = bf16[1,32,6,2048]{3,2,0,1:T(8,128)(2,1)S(1)} async-done(((bf16[1,32,6,2048]{3,2,0,1:T(8,128)(2,1)}), bf16[1,32,6,2048]{3,2,0,1:T(8,128)(2,1)S(1)}, u32[]{:S(2)}, u32[]{:S(2)}) %all-to-all-start) | async-done | bytes 786464 | tf_op jit(solution)/shard_map/while/body/eval_jaxpr/all_to_all | solution.py:103
  846.2 5.0 all-to-all-start.1
  851.5 24.7 %all-to-all-done.1 = bf16[1,32,6,2048]{3,2,0,1:T(8,128)(2,1)S(1)} async-done(((bf16[1,32,6,2048]{3,2,0,1:T(8,128)(2,1)}), bf16[1,32,6,2048]{3,2,0,1:T(8,128)(2,1)S(1)}, u32[]{:S(2)}, u32[]{:S(2)}) %all-to-all-start.1) | async-done | bytes 786464 | tf_op jit(solution)/shard_map/while/body/eval_jaxpr/all_to_all | solution.py:114
  876.6 7.8 gather_fusion.1
  887.7 12.9 %collective-permute-done = bf16[1,64,2048]{2,1,0:T(8,128)(2,1)S(1)} collective-permute-done((bf16[1,64,2048]{2,1,0:T(8,128)(2,1)S(1)}, bf16[1,64,2048]{2,1,0:T(8,128)(2,1)S(1)}, u32[]{:S(2)}, u32[]{:S(2)}) %collective-permute-start) | collective-permute-done | bytes 262176 | tf_op jit(solution)/shard_map/while/body/eval_jaxpr/ppermute | solution.py:16
  (281 shorter events, 136.3 us)
Async XLA Ops:
  1.2 1.2 copy-start.3
  1.6 1.1 copy-start.4
  1.6 1.1 copy-start.5
  1.7 5.7 copy-start.2
  21.0 48.0 %all-to-all-start.2 = ((bf16[2,32,6,2048]{3,0,2,1:T(2,128)(2,1)}), bf16[2,32,6,2048]{3,0,2,1:T(2,128)(2,1)S(1)}, u32[]{:S(2)}, u32[]{:S(2)}) async-start(bf16[2,32,6,2048]{3,0,2,1:T(2,128)(2,1)} %copy.48), calls=%async_computation.2 | async-start | bytes 3145728 | tf_op jit(solution)/shard_map/all_to_all | solution.py:92
  69.0 5.8 copy-start.6
  85.8 32.4 %all-to-all-start = ((bf16[1,32,6,2048]{3,2,0,1:T(8,128)(2,1)}), bf16[1,32,6,2048]{3,2,0,1:T(8,128)(2,1)S(1)}, u32[]{:S(2)}, u32[]{:S(2)}) async-start(bf16[1,32,6,2048]{3,2,0,1:T(8,128)(2,1)} %bitcast.143), calls=%async_computation | async-start | bytes 2097152 | tf_op jit(solution)/shard_map/while/body/eval_jaxpr/all_to_all | solution.py:103
  119.8 33.2 %all-to-all-start.1 = ((bf16[1,32,6,2048]{3,2,0,1:T(8,128)(2,1)}), bf16[1,32,6,2048]{3,2,0,1:T(8,128)(2,1)S(1)}, u32[]{:S(2)}, u32[]{:S(2)}) async-start(bf16[1,32,6,2048]{3,2,0,1:T(8,128)(2,1)} %copy.76), calls=%async_computation.1 | async-start | bytes 2097152 | tf_op jit(solution)/shard_map/while/body/eval_jaxpr/all_to_all | solution.py:114
  161.2 1.0 copy-start
  162.5 12.1 %copy-start.1 = (bf16[2,64,2048]{2,1,0:T(8,128)(2,1)}, bf16[2,64,2048]{2,1,0:T(8,128)(2,1)S(1)}, u32[]{:S(2)}) copy-start(bf16[2,64,2048]{2,1,0:T(8,128)(2,1)S(1)} %get-tuple-element.596) | copy-start | bytes 1572868 | tf_op jit(solution)/shard_map/while
  162.5 12.1 %collective-permute-start = (bf16[1,64,2048]{2,1,0:T(8,128)(2,1)S(1)}, bf16[1,64,2048]{2,1,0:T(8,128)(2,1)S(1)}, u32[]{:S(2)}, u32[]{:S(2)}) collective-permute-start(bf16[1,64,2048]{2,1,0:T(8,128)(2,1)S(1)} %get-tuple-element.556), channel_id=1, source_target_pairs={{32,0},{64,32},{96,64},{128,96},{160,128},{192,160},{224,192},{33,... | collective-permute-start | bytes 786440 | tf_op jit(solution)/shard_map/while/body/eval_jaxpr/ppermute | solution.py:16
  180.9 32.7 %all-to-all-start = ((bf16[1,32,6,2048]{3,2,0,1:T(8,128)(2,1)}), bf16[1,32,6,2048]{3,2,0,1:T(8,128)(2,1)S(1)}, u32[]{:S(2)}, u32[]{:S(2)}) async-start(bf16[1,32,6,2048]{3,2,0,1:T(8,128)(2,1)} %bitcast.143), calls=%async_computation | async-start | bytes 2097152 | tf_op jit(solution)/shard_map/while/body/eval_jaxpr/all_to_all | solution.py:103
  215.2 30.4 %all-to-all-start.1 = ((bf16[1,32,6,2048]{3,2,0,1:T(8,128)(2,1)}), bf16[1,32,6,2048]{3,2,0,1:T(8,128)(2,1)S(1)}, u32[]{:S(2)}, u32[]{:S(2)}) async-start(bf16[1,32,6,2048]{3,2,0,1:T(8,128)(2,1)} %copy.76), calls=%async_computation.1 | async-start | bytes 2097152 | tf_op jit(solution)/shard_map/while/body/eval_jaxpr/all_to_all | solution.py:114
  253.7 1.0 copy-start
  255.1 11.7 %copy-start.1 = (bf16[2,64,2048]{2,1,0:T(8,128)(2,1)}, bf16[2,64,2048]{2,1,0:T(8,128)(2,1)S(1)}, u32[]{:S(2)}) copy-start(bf16[2,64,2048]{2,1,0:T(8,128)(2,1)S(1)} %get-tuple-element.596) | copy-start | bytes 1572868 | tf_op jit(solution)/shard_map/while
  255.1 11.7 %collective-permute-start = (bf16[1,64,2048]{2,1,0:T(8,128)(2,1)S(1)}, bf16[1,64,2048]{2,1,0:T(8,128)(2,1)S(1)}, u32[]{:S(2)}, u32[]{:S(2)}) collective-permute-start(bf16[1,64,2048]{2,1,0:T(8,128)(2,1)S(1)} %get-tuple-element.556), channel_id=1, source_target_pairs={{32,0},{64,32},{96,64},{128,96},{160,128},{192,160},{224,192},{33,... | collective-permute-start | bytes 786440 | tf_op jit(solution)/shard_map/while/body/eval_jaxpr/ppermute | solution.py:16
  273.1 32.8 %all-to-all-start = ((bf16[1,32,6,2048]{3,2,0,1:T(8,128)(2,1)}), bf16[1,32,6,2048]{3,2,0,1:T(8,128)(2,1)S(1)}, u32[]{:S(2)}, u32[]{:S(2)}) async-start(bf16[1,32,6,2048]{3,2,0,1:T(8,128)(2,1)} %bitcast.143), calls=%async_computation | async-start | bytes 2097152 | tf_op jit(solution)/shard_map/while/body/eval_jaxpr/all_to_all | solution.py:103
  307.5 30.1 %all-to-all-start.1 = ((bf16[1,32,6,2048]{3,2,0,1:T(8,128)(2,1)}), bf16[1,32,6,2048]{3,2,0,1:T(8,128)(2,1)S(1)}, u32[]{:S(2)}, u32[]{:S(2)}) async-start(bf16[1,32,6,2048]{3,2,0,1:T(8,128)(2,1)} %copy.76), calls=%async_computation.1 | async-start | bytes 2097152 | tf_op jit(solution)/shard_map/while/body/eval_jaxpr/all_to_all | solution.py:114
  345.8 1.0 copy-start
  347.1 7.7 copy-start.1
  347.1 7.7 collective-permute-start
  361.2 36.0 %all-to-all-start = ((bf16[1,32,6,2048]{3,2,0,1:T(8,128)(2,1)}), bf16[1,32,6,2048]{3,2,0,1:T(8,128)(2,1)S(1)}, u32[]{:S(2)}, u32[]{:S(2)}) async-start(bf16[1,32,6,2048]{3,2,0,1:T(8,128)(2,1)} %bitcast.143), calls=%async_computation | async-start | bytes 2097152 | tf_op jit(solution)/shard_map/while/body/eval_jaxpr/all_to_all | solution.py:103
  398.7 31.4 %all-to-all-start.1 = ((bf16[1,32,6,2048]{3,2,0,1:T(8,128)(2,1)}), bf16[1,32,6,2048]{3,2,0,1:T(8,128)(2,1)S(1)}, u32[]{:S(2)}, u32[]{:S(2)}) async-start(bf16[1,32,6,2048]{3,2,0,1:T(8,128)(2,1)} %copy.76), calls=%async_computation.1 | async-start | bytes 2097152 | tf_op jit(solution)/shard_map/while/body/eval_jaxpr/all_to_all | solution.py:114
  438.2 1.0 copy-start
  439.5 19.2 %copy-start.1 = (bf16[2,64,2048]{2,1,0:T(8,128)(2,1)}, bf16[2,64,2048]{2,1,0:T(8,128)(2,1)S(1)}, u32[]{:S(2)}) copy-start(bf16[2,64,2048]{2,1,0:T(8,128)(2,1)S(1)} %get-tuple-element.596) | copy-start | bytes 1572868 | tf_op jit(solution)/shard_map/while
  439.6 19.2 %collective-permute-start = (bf16[1,64,2048]{2,1,0:T(8,128)(2,1)S(1)}, bf16[1,64,2048]{2,1,0:T(8,128)(2,1)S(1)}, u32[]{:S(2)}, u32[]{:S(2)}) collective-permute-start(bf16[1,64,2048]{2,1,0:T(8,128)(2,1)S(1)} %get-tuple-element.556), channel_id=1, source_target_pairs={{32,0},{64,32},{96,64},{128,96},{160,128},{192,160},{224,192},{33,... | collective-permute-start | bytes 786440 | tf_op jit(solution)/shard_map/while/body/eval_jaxpr/ppermute | solution.py:16
  465.1 25.1 %all-to-all-start = ((bf16[1,32,6,2048]{3,2,0,1:T(8,128)(2,1)}), bf16[1,32,6,2048]{3,2,0,1:T(8,128)(2,1)S(1)}, u32[]{:S(2)}, u32[]{:S(2)}) async-start(bf16[1,32,6,2048]{3,2,0,1:T(8,128)(2,1)} %bitcast.143), calls=%async_computation | async-start | bytes 2097152 | tf_op jit(solution)/shard_map/while/body/eval_jaxpr/all_to_all | solution.py:103
  490.2 3.6 copy-start.7
  493.8 2.5 copy-start.8
  500.2 22.1 %all-to-all-start.1 = ((bf16[1,32,6,2048]{3,2,0,1:T(8,128)(2,1)}), bf16[1,32,6,2048]{3,2,0,1:T(8,128)(2,1)S(1)}, u32[]{:S(2)}, u32[]{:S(2)}) async-start(bf16[1,32,6,2048]{3,2,0,1:T(8,128)(2,1)} %copy.76), calls=%async_computation.1 | async-start | bytes 2097152 | tf_op jit(solution)/shard_map/while/body/eval_jaxpr/all_to_all | solution.py:114
  530.5 1.0 copy-start
  531.8 19.4 %copy-start.1 = (bf16[2,64,2048]{2,1,0:T(8,128)(2,1)}, bf16[2,64,2048]{2,1,0:T(8,128)(2,1)S(1)}, u32[]{:S(2)}) copy-start(bf16[2,64,2048]{2,1,0:T(8,128)(2,1)S(1)} %get-tuple-element.596) | copy-start | bytes 1572868 | tf_op jit(solution)/shard_map/while
  531.8 19.4 %collective-permute-start = (bf16[1,64,2048]{2,1,0:T(8,128)(2,1)S(1)}, bf16[1,64,2048]{2,1,0:T(8,128)(2,1)S(1)}, u32[]{:S(2)}, u32[]{:S(2)}) collective-permute-start(bf16[1,64,2048]{2,1,0:T(8,128)(2,1)S(1)} %get-tuple-element.556), channel_id=1, source_target_pairs={{32,0},{64,32},{96,64},{128,96},{160,128},{192,160},{224,192},{33,... | collective-permute-start | bytes 786440 | tf_op jit(solution)/shard_map/while/body/eval_jaxpr/ppermute | solution.py:16
  557.5 22.1 %all-to-all-start = ((bf16[1,32,6,2048]{3,2,0,1:T(8,128)(2,1)}), bf16[1,32,6,2048]{3,2,0,1:T(8,128)(2,1)S(1)}, u32[]{:S(2)}, u32[]{:S(2)}) async-start(bf16[1,32,6,2048]{3,2,0,1:T(8,128)(2,1)} %bitcast.143), calls=%async_computation | async-start | bytes 2097152 | tf_op jit(solution)/shard_map/while/body/eval_jaxpr/all_to_all | solution.py:103
  579.6 3.6 copy-start.7
  583.2 2.5 copy-start.8
  589.6 21.8 %all-to-all-start.1 = ((bf16[1,32,6,2048]{3,2,0,1:T(8,128)(2,1)}), bf16[1,32,6,2048]{3,2,0,1:T(8,128)(2,1)S(1)}, u32[]{:S(2)}, u32[]{:S(2)}) async-start(bf16[1,32,6,2048]{3,2,0,1:T(8,128)(2,1)} %copy.76), calls=%async_computation.1 | async-start | bytes 2097152 | tf_op jit(solution)/shard_map/while/body/eval_jaxpr/all_to_all | solution.py:114
  619.6 1.0 copy-start
  620.9 16.0 %copy-start.1 = (bf16[2,64,2048]{2,1,0:T(8,128)(2,1)}, bf16[2,64,2048]{2,1,0:T(8,128)(2,1)S(1)}, u32[]{:S(2)}) copy-start(bf16[2,64,2048]{2,1,0:T(8,128)(2,1)S(1)} %get-tuple-element.596) | copy-start | bytes 1572868 | tf_op jit(solution)/shard_map/while
  620.9 16.0 %collective-permute-start = (bf16[1,64,2048]{2,1,0:T(8,128)(2,1)S(1)}, bf16[1,64,2048]{2,1,0:T(8,128)(2,1)S(1)}, u32[]{:S(2)}, u32[]{:S(2)}) collective-permute-start(bf16[1,64,2048]{2,1,0:T(8,128)(2,1)S(1)} %get-tuple-element.556), channel_id=1, source_target_pairs={{32,0},{64,32},{96,64},{128,96},{160,128},{192,160},{224,192},{33,... | collective-permute-start | bytes 786440 | tf_op jit(solution)/shard_map/while/body/eval_jaxpr/ppermute | solution.py:16
  643.3 24.1 %all-to-all-start = ((bf16[1,32,6,2048]{3,2,0,1:T(8,128)(2,1)}), bf16[1,32,6,2048]{3,2,0,1:T(8,128)(2,1)S(1)}, u32[]{:S(2)}, u32[]{:S(2)}) async-start(bf16[1,32,6,2048]{3,2,0,1:T(8,128)(2,1)} %bitcast.143), calls=%async_computation | async-start | bytes 2097152 | tf_op jit(solution)/shard_map/while/body/eval_jaxpr/all_to_all | solution.py:103
  668.9 29.7 %all-to-all-start.1 = ((bf16[1,32,6,2048]{3,2,0,1:T(8,128)(2,1)}), bf16[1,32,6,2048]{3,2,0,1:T(8,128)(2,1)S(1)}, u32[]{:S(2)}, u32[]{:S(2)}) async-start(bf16[1,32,6,2048]{3,2,0,1:T(8,128)(2,1)} %copy.76), calls=%async_computation.1 | async-start | bytes 2097152 | tf_op jit(solution)/shard_map/while/body/eval_jaxpr/all_to_all | solution.py:114
  706.8 1.0 copy-start
  708.1 15.3 %copy-start.1 = (bf16[2,64,2048]{2,1,0:T(8,128)(2,1)}, bf16[2,64,2048]{2,1,0:T(8,128)(2,1)S(1)}, u32[]{:S(2)}) copy-start(bf16[2,64,2048]{2,1,0:T(8,128)(2,1)S(1)} %get-tuple-element.596) | copy-start | bytes 1572868 | tf_op jit(solution)/shard_map/while
  708.2 15.3 %collective-permute-start = (bf16[1,64,2048]{2,1,0:T(8,128)(2,1)S(1)}, bf16[1,64,2048]{2,1,0:T(8,128)(2,1)S(1)}, u32[]{:S(2)}, u32[]{:S(2)}) collective-permute-start(bf16[1,64,2048]{2,1,0:T(8,128)(2,1)S(1)} %get-tuple-element.556), channel_id=1, source_target_pairs={{32,0},{64,32},{96,64},{128,96},{160,128},{192,160},{224,192},{33,... | collective-permute-start | bytes 786440 | tf_op jit(solution)/shard_map/while/body/eval_jaxpr/ppermute | solution.py:16
  729.8 28.8 %all-to-all-start = ((bf16[1,32,6,2048]{3,2,0,1:T(8,128)(2,1)}), bf16[1,32,6,2048]{3,2,0,1:T(8,128)(2,1)S(1)}, u32[]{:S(2)}, u32[]{:S(2)}) async-start(bf16[1,32,6,2048]{3,2,0,1:T(8,128)(2,1)} %bitcast.143), calls=%async_computation | async-start | bytes 2097152 | tf_op jit(solution)/shard_map/while/body/eval_jaxpr/all_to_all | solution.py:103
  760.1 30.6 %all-to-all-start.1 = ((bf16[1,32,6,2048]{3,2,0,1:T(8,128)(2,1)}), bf16[1,32,6,2048]{3,2,0,1:T(8,128)(2,1)S(1)}, u32[]{:S(2)}, u32[]{:S(2)}) async-start(bf16[1,32,6,2048]{3,2,0,1:T(8,128)(2,1)} %copy.76), calls=%async_computation.1 | async-start | bytes 2097152 | tf_op jit(solution)/shard_map/while/body/eval_jaxpr/all_to_all | solution.py:114
  799.0 1.0 copy-start
  800.3 10.7 %copy-start.1 = (bf16[2,64,2048]{2,1,0:T(8,128)(2,1)}, bf16[2,64,2048]{2,1,0:T(8,128)(2,1)S(1)}, u32[]{:S(2)}) copy-start(bf16[2,64,2048]{2,1,0:T(8,128)(2,1)S(1)} %get-tuple-element.596) | copy-start | bytes 1572868 | tf_op jit(solution)/shard_map/while
  800.3 10.6 %collective-permute-start = (bf16[1,64,2048]{2,1,0:T(8,128)(2,1)S(1)}, bf16[1,64,2048]{2,1,0:T(8,128)(2,1)S(1)}, u32[]{:S(2)}, u32[]{:S(2)}) collective-permute-start(bf16[1,64,2048]{2,1,0:T(8,128)(2,1)S(1)} %get-tuple-element.556), channel_id=1, source_target_pairs={{32,0},{64,32},{96,64},{128,96},{160,128},{192,160},{224,192},{33,... | collective-permute-start | bytes 786440 | tf_op jit(solution)/shard_map/while/body/eval_jaxpr/ppermute | solution.py:16
  817.3 27.4 %all-to-all-start = ((bf16[1,32,6,2048]{3,2,0,1:T(8,128)(2,1)}), bf16[1,32,6,2048]{3,2,0,1:T(8,128)(2,1)S(1)}, u32[]{:S(2)}, u32[]{:S(2)}) async-start(bf16[1,32,6,2048]{3,2,0,1:T(8,128)(2,1)} %bitcast.143), calls=%async_computation | async-start | bytes 2097152 | tf_op jit(solution)/shard_map/while/body/eval_jaxpr/all_to_all | solution.py:103
  846.2 30.0 %all-to-all-start.1 = ((bf16[1,32,6,2048]{3,2,0,1:T(8,128)(2,1)}), bf16[1,32,6,2048]{3,2,0,1:T(8,128)(2,1)S(1)}, u32[]{:S(2)}, u32[]{:S(2)}) async-start(bf16[1,32,6,2048]{3,2,0,1:T(8,128)(2,1)} %copy.76), calls=%async_computation.1 | async-start | bytes 2097152 | tf_op jit(solution)/shard_map/while/body/eval_jaxpr/all_to_all | solution.py:114
  884.4 1.0 copy-start
  885.7 14.8 %copy-start.1 = (bf16[2,64,2048]{2,1,0:T(8,128)(2,1)}, bf16[2,64,2048]{2,1,0:T(8,128)(2,1)S(1)}, u32[]{:S(2)}) copy-start(bf16[2,64,2048]{2,1,0:T(8,128)(2,1)S(1)} %get-tuple-element.596) | copy-start | bytes 1572868 | tf_op jit(solution)/shard_map/while
  885.7 14.8 %collective-permute-start = (bf16[1,64,2048]{2,1,0:T(8,128)(2,1)S(1)}, bf16[1,64,2048]{2,1,0:T(8,128)(2,1)S(1)}, u32[]{:S(2)}, u32[]{:S(2)}) collective-permute-start(bf16[1,64,2048]{2,1,0:T(8,128)(2,1)S(1)} %get-tuple-element.556), channel_id=1, source_target_pairs={{32,0},{64,32},{96,64},{128,96},{160,128},{192,160},{224,192},{33,... | collective-permute-start | bytes 786440 | tf_op jit(solution)/shard_map/while/body/eval_jaxpr/ppermute | solution.py:16
where the time goes:
time: 904 us; the launch traced here: 901 us
  waiting for transfers between devices  544 us (60%)
  local copies, waits for them, and re-layouts  160 us (18%)
  starting transfers between devices  149 us (16%)
  matrix products  32.8 us (4%)
  other arithmetic  13 us (1%)
    all_to_all x9, waiting for transfers between devices, run_group(): lax.all_to_all(grad_rows, 'expert', split_axis=1, concat_axis=1, tiled=True)  212 us
    all_to_all x9, waiting for transfers between devices, run_group(): lax.all_to_all(local_rows, 'expert', split_axis=1, concat_axis=1, tiled=T...  208 us
    ppermute x9, waiting for transfers between devices, from_behind(): return lax.ppermute(shard, axis, pairs)  87.5 us
    gather x27, local copies, waits for them, and re-layouts, combine_rows(): picked = padded[slot_place].astype(jnp.float32)  71.3 us
    all_to_all x9, starting transfers between devices, run_group(): lax.all_to_all(grad_rows, 'expert', split_axis=1, concat_axis=1, tiled=True)  49.5 us
    all_to_all x9, starting transfers between devices, run_group(): lax.all_to_all(local_rows, 'expert', split_axis=1, concat_axis=1, tiled=T...  49 us
    gather x20, local copies, waits for them, and re-layouts, dispatch_rows(): return padded[slot_owner]  44 us
    ppermute x9, starting transfers between devices, from_behind(): return lax.ppermute(shard, axis, pairs)  39 us
  transfers between devices with their start and end apart: 28, of which 28 were waited for; matrix products, arithmetic and copies ran while one was open for 0% of the time, Pallas kernels for 0%

commit v1 on v0

v1 whole, which is shorter than its diff:
```python
from functools import partial

import jax
import jax.numpy as jnp
from jax import lax
from jax.experimental import pallas as pl
from jax.experimental.pallas import tpu as pltpu
from jax.sharding import PartitionSpec as P

CAP = 6
PAD = 8
MESH = pl.DeviceIdType.MESH
F32 = jnp.float32
BF16 = jnp.bfloat16
NT = (((1,), (1,)), ((), ()))


def dot(a, b):
    return jnp.dot(a, b, preferred_element_type=F32)


def dot_nt(a, b):
    return lax.dot_general(a, b, NT, preferred_element_type=F32)


def kernel(
    sizes,
    acts,
    out_grad,
    w_gate,
    w_up,
    w_down,
    routes,
    gates,
    result,
    gate_w,
    up_w,
    down_w,
    own_acts,
    incoming,
    finished,
    own_pick,
    next_pick,
    blend,
    act_out,
    act_in,
    seed_out,
    grad_out,
    grad_in,
    row_out,
    row_in,
    stage,
    gate_coef,
    up_coef,
    hidden,
    weight_sem,
    load_sem,
    store_sem,
    pick_send,
    pick_recv,
    pass_send,
    pass_recv,
    act_send,
    act_recv,
    seed_send,
    grad_send,
    grad_recv,
    row_send,
    row_recv,
):
    sections, live, micro, tokens, width, chunks = sizes
    part = width // chunks
    slots = live * PAD
    section = lax.axis_index("pipe")
    mine = lax.axis_index("expert")
    first = section == sections - 1
    last = section == 0

    def local(src, dst, sem):
        return pltpu.make_async_copy(src, dst, sem)

    def arrived(ref, sem):
        pltpu.make_async_copy(ref, ref, sem).wait()

    def columns(c):
        return pl.ds(c * part, part)

    loads = [
        local(w_gate.at[0, 0], gate_w, weight_sem.at[0]),
        local(w_up.at[0, 0], up_w, weight_sem.at[1]),
        local(w_down.at[0, 0], down_w, weight_sem.at[2]),
    ]
    act_loads = [local(acts.at[0, m], own_acts.at[m], load_sem.at[m]) for m in range(micro)]
    for m in range(micro):
        act_loads[m].start()

    @pl.when(first)
    def _():
        for m in range(micro):
            local(out_grad.at[m], incoming.at[m], pass_recv.at[m]).start()

    for load in loads:
        load.start()

    stage[...] = jnp.zeros_like(stage)

    expert_of = lax.broadcasted_iota(jnp.int32, (tokens, live), 1)
    earlier = (
        lax.broadcasted_iota(jnp.int32, (tokens, tokens), 1)
        < lax.broadcasted_iota(jnp.int32, (tokens, tokens), 0)
    ).astype(F32).astype(BF16)
    spread = (
        lax.shift_right_logical(lax.broadcasted_iota(jnp.int32, (live, slots), 1), 3)
        == lax.broadcasted_iota(jnp.int32, (live, slots), 0)
    ).astype(F32)
    lane = lax.bitwise_and(lax.broadcasted_iota(jnp.int32, (tokens, slots), 1), PAD - 1)
    for m in range(micro):
        chosen = jnp.zeros((tokens, live), F32)
        weight = jnp.zeros((tokens, live), F32)
        for k in range(routes.shape[-1]):
            hit = routes[0, m, :, k : k + 1] == expert_of
            chosen = chosen + jnp.where(hit, 1.0, 0.0)
            weight = weight + jnp.where(hit, gates[0, m, :, k : k + 1], 0.0)
        slot = dot(earlier, chosen.astype(BF16))
        slot = dot(slot.astype(BF16), spread.astype(BF16))
        chosen = dot(chosen.astype(BF16), spread.astype(BF16))
        weight = jnp.dot(weight, spread, preferred_element_type=F32, precision=lax.Precision.HIGHEST)
        kept = (chosen > 0.5) & (jnp.abs(slot - lane.astype(F32)) < 0.5) & (lane < CAP)
        weight = jnp.where(kept, weight, 0.0)
        high = weight.astype(BF16)
        blend[m, 0:tokens, :] = high
        blend[m, tokens : 2 * tokens, :] = (weight - high.astype(F32)).astype(BF16)
        own_pick[m] = jnp.where(kept, 1.0, 0.0).T.astype(BF16)

    pick_copy = pltpu.make_async_remote_copy(
        own_pick,
        next_pick,
        pick_send,
        pick_recv,
        device_id=(jnp.minimum(section + 1, sections - 1), mine),
        device_id_type=MESH,
    )

    @pl.when(jnp.logical_not(first))
    def _():
        pick_copy.start()

    def send_slots(src, dst, m, c, target_section, send_sem, recv_sem, own):
        def one(i, carry):
            target = lax.rem(mine + i, live)
            pltpu.make_async_remote_copy(
                src.at[m, c, target],
                dst.at[m, c, mine],
                send_sem.at[m],
                recv_sem.at[m, c],
                device_id=(target_section, target),
                device_id_type=MESH,
            ).start()
            return carry

        if own:
            local(src.at[m, c, mine], dst.at[m, c, mine], recv_sem.at[m, c]).start()
        lax.fori_loop(1 if own else 0, live, one, 0)

    def sent(src, m, send_sem, own):
        for c in range(chunks):
            ref = src.at[m, c, pl.ds(0, live - 1)] if own else src.at[m, c]
            arrived(ref, send_sem.at[m])

    def put(dst, m, c, rows):
        dst[m, c] = rows.reshape(live, PAD, part)[:, :CAP, :].astype(BF16)

    def take(src, m, c):
        stage[c % 2, :, 0:CAP, :] = src[m, c].astype(F32)
        return stage[c % 2].reshape(slots, part).astype(BF16)

    for m in range(micro):
        act_loads[m].wait()
        for c in range(chunks):
            put(act_out, m, c, dot(own_pick[m], own_acts[m, :, columns(c)]))
            send_slots(act_out, act_in, m, c, section, act_send, act_recv, True)

        @pl.when(first)
        def _():
            arrived(incoming.at[m], pass_recv.at[m])
            for c in range(chunks):
                put(seed_out, m, c, dot(own_pick[m], incoming[m, :, columns(c)]))
                send_slots(seed_out, grad_in, m, c, section, seed_send, grad_recv, True)

    for load in loads:
        load.wait()

    def coefficients(m, carry):
        for c in range(chunks):
            arrived(act_in.at[m, c], act_recv.at[m, c])
            rows = take(act_in, m, c)
            gate_part = dot(rows, gate_w[columns(c), :])
            up_part = dot(rows, up_w[columns(c), :])
            if c == 0:
                gate_coef[m] = gate_part
                up_coef[m] = up_part
            else:
                gate_coef[m] += gate_part
                up_coef[m] += up_part
        gate_pre = gate_coef[m]
        up_pre = up_coef[m]
        sigmoid_gate = 1.0 / (1.0 + jnp.exp(-gate_pre))
        gate_coef[m] = up_pre * sigmoid_gate * (1.0 + gate_pre * (1.0 - sigmoid_gate))
        up_coef[m] = gate_pre * sigmoid_gate
        return carry

    lax.fori_loop(0, micro, coefficients, 0)

    @pl.when(jnp.logical_not(last))
    def _():
        arrived(next_pick, pick_recv)

    def step(m, carry):
        for c in range(chunks):
            arrived(grad_in.at[m, c], grad_recv.at[m, c])
            hidden_part = dot_nt(take(grad_in, m, c), down_w[:, columns(c)])
            if c == 0:
                hidden[...] = hidden_part
            else:
                hidden[...] += hidden_part
        hidden_grad = hidden[...]
        gate_grad = (hidden_grad * gate_coef[m]).astype(BF16)
        up_grad = (hidden_grad * up_coef[m]).astype(BF16)
        for c in range(chunks):
            rows = dot_nt(gate_grad, gate_w[columns(c), :]) + dot_nt(up_grad, up_w[columns(c), :])
            put(row_out, m, c, rows)
            send_slots(row_out, row_in, m, c, section, row_send, row_recv, True)

        @pl.when(jnp.logical_not(first))
        def _():
            arrived(incoming.at[m], pass_recv.at[m])

        for c in range(chunks):
            arrived(row_in.at[m, c], row_recv.at[m, c])
            both = dot(blend[m], take(row_in, m, c))
            total = incoming[m, :, columns(c)].astype(F32) + (both[:tokens] + both[tokens:])
            total = total.astype(BF16)
            finished[m, :, columns(c)] = total

            @pl.when(jnp.logical_not(last))
            def _():
                put(grad_out, m, c, dot(next_pick[m], total))
                send_slots(grad_out, grad_in, m, c, section - 1, grad_send, grad_recv, False)

        @pl.when(jnp.logical_not(last))
        def _():
            pltpu.make_async_remote_copy(
                finished.at[m],
                incoming.at[m],
                pass_send.at[m],
                pass_recv.at[m],
                device_id=(section - 1, mine),
                device_id_type=MESH,
            ).start()

        local(finished.at[m], result.at[0, m], store_sem.at[m]).start()
        return carry

    lax.fori_loop(0, micro, step, 0)

    @pl.when(jnp.logical_not(first))
    def _():
        pick_copy.wait_send()

    for m in range(micro):
        sent(act_out, m, act_send, True)
        sent(row_out, m, row_send, True)
        arrived(finished.at[m], store_sem.at[m])

        @pl.when(first)
        def _():
            sent(seed_out, m, seed_send, True)

        @pl.when(jnp.logical_not(last))
        def _():
            arrived(finished.at[m], pass_send.at[m])
            sent(grad_out, m, grad_send, False)


def shards(chunks, acts, out_grad, w_gate, w_up, w_down, routes, gates):
    sections = lax.axis_size("pipe")
    live = lax.axis_size("expert")
    micro, tokens, width = acts.shape[1:]
    units = w_gate.shape[-1]
    part = width // chunks
    slots = live * PAD
    sizes = (sections, live, micro, tokens, width, chunks)
    slab = pltpu.VMEM((micro, chunks, live, CAP, part), BF16)
    block = pltpu.VMEM((micro, tokens, width), BF16)
    sems = pltpu.SemaphoreType.DMA((micro,))
    chunk_sems = pltpu.SemaphoreType.DMA((micro, chunks))
    whole = pl.BlockSpec(memory_space=pltpu.VMEM)
    place = pl.BlockSpec(memory_space=pl.ANY)
    return pl.pallas_call(
        partial(kernel, sizes),
        out_shape=jax.ShapeDtypeStruct(acts.shape, BF16),
        in_specs=[place] * 5 + [whole] * 2,
        out_specs=place,
        scratch_shapes=[
            pltpu.VMEM((width, units), BF16),
            pltpu.VMEM((width, units), BF16),
            pltpu.VMEM((units, width), BF16),
            block,
            block,
            block,
            pltpu.VMEM((micro, slots, tokens), BF16),
            pltpu.VMEM((micro, slots, tokens), BF16),
            pltpu.VMEM((micro, 2 * tokens, slots), BF16),
            slab,
            slab,
            slab,
            slab,
            slab,
            slab,
            slab,
            pltpu.VMEM((2, live, PAD, part), F32),
            pltpu.VMEM((micro, slots, units), F32),
            pltpu.VMEM((micro, slots, units), F32),
            pltpu.VMEM((slots, units), F32),
            pltpu.SemaphoreType.DMA((3,)),
            sems,
            sems,
            pltpu.SemaphoreType.DMA,
            pltpu.SemaphoreType.DMA,
            sems,
            sems,
            sems,
            chunk_sems,
            sems,
            sems,
            chunk_sems,
            sems,
            chunk_sems,
        ],
        compiler_params=pltpu.CompilerParams(
            has_side_effects=True, vmem_limit_bytes=60 * 1024 * 1024
        ),
    )(acts, out_grad, w_gate, w_up, w_down, routes, gates)


def solution(mesh, chunks=4):
    return jax.shard_map(
        partial(shards, chunks),
        mesh=mesh,
        in_specs=(
            P("pipe", None, "expert", None),
            P(None, "expert", None),
            P("pipe", "expert", None, None),
            P("pipe", "expert", None, None),
            P("pipe", "expert", None, None),
            P("pipe", None, "expert", None),
            P("pipe", None, "expert", None),
        ),
        out_specs=P("pipe", None, "expert", None),
        check_vma=False,
    )
```

time: 904 us -> 394 us (0.44)
  the two profiles are of different devices: /device:TPU:3 before, /device:TPU:24 now
where the time goes in v1:
time: 394 us
  Pallas kernels  389 us (99%)
  local copies, waits for them, and re-layouts  4.72 us (1%)
    pallas_call x1, Pallas kernels, shards(): pl.pallas_call(partial(kernel, sizes), out_shape=jax.ShapeDtypeStruct(act...  389 us

profile of v1, /device:TPU:24, one launch (start us, length us, event | category | flops | bytes accessed | tf_op | source)
XLA Modules:
  0.0 393.8 jit_solution(6596519396673758154)
XLA Ops:
  0.0 1.4 copy.8.routes
  1.4 1.4 copy.9.gates
  2.8 389.1 %shard_map.73 = bf16[1,2,64,2048]{3,2,1,0:T(8,128)(2,1)} custom-call(bf16[1,2,64,2048]{3,2,1,0:T(8,128)(2,1)} %acts.1, bf16[2,64,2048]{2,1,0:T(8,128)(2,1)} %out_grad.1, bf16[1,1,2048,768]{3,2,1,0:T(8,128)(2,1)} %w_gate.1, bf16[1,1,2048,768]{3,2,1,0:T(8,128)(2,1)} %w_up.1, bf16[1,1,768,2048]{3,2,1,0:T(8,128)(2,1)} %w_down.1, s32[1,2,64,8]{3,2,1,0:T(8,128)} %copy.8.routes, ...), custom_call_target="tpu_custom_call" | custom-call | tf_op jit(solution)/shard_map/pallas_call | solution.py:299
  391.9 1.9 copy.11

commit v2 on v1

--- a/solution.py
+++ b/solution.py
@@ -9,6 +9,7 @@
 
 CAP = 6
 PAD = 8
+LANES = 128
 MESH = pl.DeviceIdType.MESH
 F32 = jnp.float32
 BF16 = jnp.bfloat16
@@ -49,7 +50,6 @@
     grad_in,
     row_out,
     row_in,
-    stage,
     gate_coef,
     up_coef,
     hidden,
@@ -102,7 +102,8 @@
     for load in loads:
         load.start()
 
-    stage[...] = jnp.zeros_like(stage)
+    slot_row = lax.broadcasted_iota(jnp.int32, (live, PAD, LANES), 1)
+    low_rows = slot_row < CAP
 
     expert_of = lax.broadcasted_iota(jnp.int32, (tokens, live), 1)
     earlier = (
@@ -168,11 +169,21 @@
             arrived(ref, send_sem.at[m])
 
     def put(dst, m, c, rows):
-        dst[m, c] = rows.reshape(live, PAD, part)[:, :CAP, :].astype(BF16)
+        rows = rows.reshape(live, PAD, part)
+        rest = rows[:, :, CAP // 2 * LANES :]
+        for j in range(CAP // 2):
+            moved = pltpu.roll(rest, CAP - 2 * j, 1)
+            tile = jnp.where(low_rows, rows[:, :, j * LANES : (j + 1) * LANES], moved)
+            dst[m, c, :, :, j * LANES : (j + 1) * LANES] = tile.astype(BF16)
 
     def take(src, m, c):
-        stage[c % 2, :, 0:CAP, :] = src[m, c].astype(F32)
-        return stage[c % 2].reshape(slots, part).astype(BF16)
+        packed = src[m, c].astype(F32)
+        rest = jnp.zeros((live, PAD, LANES), F32)
+        for j in range(CAP // 2):
+            moved = pltpu.roll(packed[:, :, j * LANES : (j + 1) * LANES], PAD - CAP + 2 * j, 1)
+            rest = jnp.where(slot_row // 2 == j, moved, rest)
+        rows = jnp.concatenate([packed, rest], axis=2)
+        return rows.reshape(slots, part).astype(BF16)
 
     for m in range(micro):
         act_loads[m].wait()
@@ -290,7 +301,7 @@
     part = width // chunks
     slots = live * PAD
     sizes = (sections, live, micro, tokens, width, chunks)
-    slab = pltpu.VMEM((micro, chunks, live, CAP, part), BF16)
+    slab = pltpu.VMEM((micro, chunks, live, PAD, part * CAP // PAD), BF16)
     block = pltpu.VMEM((micro, tokens, width), BF16)
     sems = pltpu.SemaphoreType.DMA((micro,))
     chunk_sems = pltpu.SemaphoreType.DMA((micro, chunks))
@@ -318,7 +329,6 @@
             slab,
             slab,
             slab,
-            pltpu.VMEM((2, live, PAD, part), F32),
             pltpu.VMEM((micro, slots, units), F32),
             pltpu.VMEM((micro, slots, units), F32),
             pltpu.VMEM((slots, units), F32),

time: 394 us -> 315 us (0.80)
  Pallas kernels: 389 us -> 309 us
    pallas_call x1, Pallas kernels: 389 us -> 309 us  [shards(): pl.pallas_call(partial(kernel, sizes), out_shape=jax.ShapeDtypeStruct(act...]
where the time goes in v2:
time: 315 us; the launch traced here: 314 us
  Pallas kernels  309 us (98%)
  local copies, waits for them, and re-layouts  4.72 us (1%)
    pallas_call x1, Pallas kernels, shards(): pl.pallas_call(partial(kernel, sizes), out_shape=jax.ShapeDtypeStruct(act...  309 us

profile of v2, /device:TPU:24, one launch (start us, length us, event | category | flops | bytes accessed | tf_op | source)
XLA Modules:
  0.0 313.7 jit_solution(5232587705019956728)
XLA Ops:
  0.0 1.4 copy.8.routes
  1.4 1.4 copy.9.gates
  2.8 309.0 %shard_map.73 = bf16[1,2,64,2048]{3,2,1,0:T(8,128)(2,1)} custom-call(bf16[1,2,64,2048]{3,2,1,0:T(8,128)(2,1)} %acts.1, bf16[2,64,2048]{2,1,0:T(8,128)(2,1)} %out_grad.1, bf16[1,1,2048,768]{3,2,1,0:T(8,128)(2,1)} %w_gate.1, bf16[1,1,2048,768]{3,2,1,0:T(8,128)(2,1)} %w_up.1, bf16[1,1,768,2048]{3,2,1,0:T(8,128)(2,1)} %w_down.1, s32[1,2,64,8]{3,2,1,0:T(8,128)} %copy.8.routes, ...), custom_call_target="tpu_custom_call" | custom-call | tf_op jit(solution)/shard_map/pallas_call | solution.py:310
  311.8 1.9 copy.11

commit v3 on v2

--- a/solution.py
+++ b/solution.py
@@ -67,6 +67,7 @@
     grad_recv,
     row_send,
     row_recv,
+    turn,
 ):
     sections, live, micro, tokens, width, chunks = sizes
     part = width // chunks
@@ -235,6 +236,11 @@
             else:
                 hidden[...] += hidden_part
         hidden_grad = hidden[...]
+
+        @pl.when((m == 1) & (lax.rem(section, 2) == 1))
+        def _():
+            pl.semaphore_wait(turn, 1)
+
         gate_grad = (hidden_grad * gate_coef[m]).astype(BF16)
         up_grad = (hidden_grad * up_coef[m]).astype(BF16)
         for c in range(chunks):
@@ -270,6 +276,11 @@
             ).start()
 
         local(finished.at[m], result.at[0, m], store_sem.at[m]).start()
+
+        @pl.when((m == 0) & (lax.rem(section, 2) == 0))
+        def _():
+            pl.semaphore_signal(turn, inc=1, device_id=(section + 1, mine), device_id_type=MESH)
+
         return carry
 
     lax.fori_loop(0, micro, step, 0)
@@ -346,6 +357,7 @@
             chunk_sems,
             sems,
             chunk_sems,
+            pltpu.SemaphoreType.REGULAR,
         ],
         compiler_params=pltpu.CompilerParams(
             has_side_effects=True, vmem_limit_bytes=60 * 1024 * 1024

time: 315 us -> 301 us (0.956)
  Pallas kernels: 309 us -> 295 us
    pallas_call x1, Pallas kernels: 309 us -> 295 us  [shards(): pl.pallas_call(partial(kernel, sizes), out_shape=jax.ShapeDtypeStruct(act...]
where the time goes in v3:
time: 301 us; the launch traced here: 300 us
  Pallas kernels  295 us (98%)
  local copies, waits for them, and re-layouts  4.72 us (2%)
    pallas_call x1, Pallas kernels, shards(): pl.pallas_call(partial(kernel, sizes), out_shape=jax.ShapeDtypeStruct(act...  295 us

profile of v3, /device:TPU:24, one launch (start us, length us, event | category | flops | bytes accessed | tf_op | source)
XLA Modules:
  0.0 300.2 jit_solution(16602222406887611548)
XLA Ops:
  0.0 1.4 copy.8.routes
  1.4 1.4 copy.9.gates
  2.8 295.5 %shard_map.73 = bf16[1,2,64,2048]{3,2,1,0:T(8,128)(2,1)} custom-call(bf16[1,2,64,2048]{3,2,1,0:T(8,128)(2,1)} %acts.1, bf16[2,64,2048]{2,1,0:T(8,128)(2,1)} %out_grad.1, bf16[1,1,2048,768]{3,2,1,0:T(8,128)(2,1)} %w_gate.1, bf16[1,1,2048,768]{3,2,1,0:T(8,128)(2,1)} %w_up.1, bf16[1,1,768,2048]{3,2,1,0:T(8,128)(2,1)} %w_down.1, s32[1,2,64,8]{3,2,1,0:T(8,128)} %copy.8.routes, ...), custom_call_target="tpu_custom_call" | custom-call | tf_op jit(solution)/shard_map/pallas_call | solution.py:321
  298.3 1.9 copy.11
